TPU v7x, 32 devices: a whole 2x2x4 slice. The times are simulated.
32 devices in a mesh: fsdp: 32 (over z, y, x, core).
Axes of the slice: x: 2, y: 2, z: 4, core: 2. Of those that a mesh axis runs over, the one named last changes fastest.
Arguments:
- block_input: bfloat16 [32, 784, 768], P('fsdp'), may hold values from -6 to 6
- seg_ids: int32 [32, 784], P('fsdp'), may hold values from 0 to 3, as said below
- gain_attn: bfloat16 [768], P('fsdp'), may hold values from 0.099609375 to 1.8984375
- w_query: bfloat16 [768, 768], P('fsdp'), may hold values from -0.21875 to 0.21875
- w_key: bfloat16 [768, 768], P('fsdp'), may hold values from -0.21875 to 0.21875
- w_value: bfloat16 [768, 768], P('fsdp'), may hold values from -0.21875 to 0.21875
- w_out: bfloat16 [768, 768], P('fsdp'), may hold values from -0.875 to 0.875
- gain_ffn: bfloat16 [768], P('fsdp'), may hold values from 0.099609375 to 1.8984375
- w_gate: bfloat16 [768, 2048], P('fsdp'), may hold values from -0.21875 to 0.21875
- w_up: bfloat16 [768, 2048], P('fsdp'), may hold values from -0.21875 to 0.21875
- w_down: bfloat16 [2048, 768], P('fsdp'), may hold values from -0.125 to 0.125
- cotangent: bfloat16 [32, 784, 768], P('fsdp'), may hold values from -6 to 6
Outputs:
- block_output: bfloat16 [32, 784, 768], P('fsdp')
- input_grad: bfloat16 [32, 784, 768], P('fsdp')
- gain_attn_grad: float32 [768], P('fsdp')
- w_query_grad: float32 [768, 768], P('fsdp')
- w_key_grad: float32 [768, 768], P('fsdp')
- w_value_grad: float32 [768, 768], P('fsdp')
- w_out_grad: float32 [768, 768], P('fsdp')
- gain_ffn_grad: float32 [768], P('fsdp')
- w_gate_grad: float32 [768, 2048], P('fsdp')
- w_up_grad: float32 [768, 2048], P('fsdp')
- w_down_grad: float32 [2048, 768], P('fsdp')
Inputs may be any that keep to these rules, and one draw needn't show every extreme that they name: `seg_ids`: each row holds, from slot 0 on, either one image of 577 tokens (segment 0) or two or three images of 257 tokens (segments 0, 1, 2 in order), and padding with segment number 3 in all remaining slots, at least one of them.
All inputs are finite; a program needn't handle non-finite values.
Results may differ from a plain program's by a relative error of at most 0.015.
Values may be sent and summed in bfloat16 or wider, within the bound.
A program may use at most 128 MiB of HBM per device.

v0:
```python
from functools import partial
import jax
import jax.numpy as jnp
from jax import lax
from jax.sharding import PartitionSpec as P

HEAD = 64
EPSILON = 1e-05


def rope_tables(segment_row, head_size):
    length = segment_row.shape[0]
    places = jnp.arange(length, dtype=jnp.int32)
    labels = jnp.arange(4, dtype=jnp.int32)
    counts = jnp.sum((segment_row[:, None] == labels[None, :]).astype(jnp.int32), axis=0)
    before = (labels[None, :] < segment_row[:, None]).astype(jnp.int32)
    starts = jnp.sum(before * counts[None, :], axis=1)
    offsets = (places - starts).astype(jnp.float32)
    frequency = 10000.0 ** (-(jnp.arange(head_size // 2, dtype=jnp.float32) * 2.0) / head_size)
    angles = offsets[:, None] * frequency[None, :]
    return (jnp.cos(angles), jnp.sin(angles))


def rotate(values, cosine, sine_table):
    half_size = values.shape[-1] // 2
    lower_half = values[..., :half_size]
    upper_half = values[..., half_size:]
    cosine = cosine[..., None, :]
    sine_table = sine_table[..., None, :]
    return jnp.concatenate(
        [
            lower_half * cosine - upper_half * sine_table,
            upper_half * cosine + lower_half * sine_table,
        ],
        axis=-1,
    )


def unrotate(gradient, cosine, sine_table):
    half_size = gradient.shape[-1] // 2
    lower_half = gradient[..., :half_size]
    upper_half = gradient[..., half_size:]
    cosine = cosine[..., None, :]
    sine_table = sine_table[..., None, :]
    return jnp.concatenate(
        [
            lower_half * cosine + upper_half * sine_table,
            upper_half * cosine - lower_half * sine_table,
        ],
        axis=-1,
    )


def head_forward(query_head, key_head, value_head, allowed, score_scale):
    raw_scores = jnp.einsum("le,me->lm", query_head, key_head, preferred_element_type=jnp.float32)
    masked = jnp.where(allowed, raw_scores * score_scale, -1e30)
    highest = jnp.max(masked, axis=-1, keepdims=True)
    exponent = jnp.exp(masked - highest)
    denominator = jnp.sum(exponent, axis=-1, keepdims=True)
    weights = (exponent / denominator).astype(jnp.bfloat16)
    mixture = jnp.dot(weights, value_head, preferred_element_type=jnp.float32)
    return (mixture, (highest + jnp.log(denominator))[:, 0])


def head_backward(query_head, key_head, value_head, grad_head, logsum, allowed, score_scale):
    raw_scores = jnp.einsum("le,me->lm", query_head, key_head, preferred_element_type=jnp.float32)
    masked = jnp.where(allowed, raw_scores * score_scale, -1e30)
    probabilities = jnp.exp(masked - logsum[:, None])
    weights = probabilities.astype(jnp.bfloat16)
    grad_value = jnp.einsum("lm,le->me", weights, grad_head, preferred_element_type=jnp.float32)
    grad_probs = jnp.einsum("le,me->lm", grad_head, value_head, preferred_element_type=jnp.float32)
    grad_scores = probabilities * (
        grad_probs - jnp.sum(grad_probs * probabilities, axis=-1, keepdims=True)
    )
    grad_scores = grad_scores.astype(jnp.bfloat16)
    grad_query = jnp.dot(grad_scores, key_head, preferred_element_type=jnp.float32) * score_scale
    grad_key = (
        jnp.einsum("lm,le->me", grad_scores, query_head, preferred_element_type=jnp.float32)
        * score_scale
    )
    return (grad_query, grad_key, grad_value)


def norm_backward(grad_normed, normed, inverse, gain):
    scaled = grad_normed * gain
    return inverse * (scaled - normed * jnp.mean(scaled * normed, axis=-1, keepdims=True))


def per_device(
    block_input,
    seg_ids,
    gain_attn,
    w_query,
    w_key,
    w_value,
    w_out,
    gain_ffn,
    w_gate,
    w_up,
    w_down,
    cotangent,
):
    row_count, length, width = block_input.shape
    head_count = width // HEAD
    tokens = row_count * length
    score_scale = HEAD ** (-0.5)
    attn_set = (
        lax.all_gather(gain_attn, "fsdp", axis=0, tiled=True),
        lax.all_gather(w_query, "fsdp", axis=0, tiled=True),
        lax.all_gather(w_key, "fsdp", axis=0, tiled=True),
        lax.all_gather(w_value, "fsdp", axis=0, tiled=True),
        lax.all_gather(w_out, "fsdp", axis=0, tiled=True),
    )
    ffn_set = (
        lax.all_gather(gain_ffn, "fsdp", axis=0, tiled=True),
        lax.all_gather(w_gate, "fsdp", axis=0, tiled=True),
        lax.all_gather(w_up, "fsdp", axis=0, tiled=True),
        lax.all_gather(w_down, "fsdp", axis=0, tiled=True),
    )
    cosine, sine_table = jax.vmap(partial(rope_tables, head_size=HEAD))(seg_ids)
    places = jnp.arange(length, dtype=jnp.int32)
    allowed = (seg_ids[:, :, None] == seg_ids[:, None, :]) & (
        places[None, None, :] <= places[None, :, None]
    )
    inputs = block_input.reshape(tokens, width).astype(jnp.float32)
    scale_one = lax.rsqrt(jnp.mean(inputs * inputs, axis=-1, keepdims=True) + EPSILON)
    normed_one = inputs * scale_one
    normed_low = (normed_one * attn_set[0].astype(jnp.float32)).astype(jnp.bfloat16)
    queries = jnp.dot(normed_low, attn_set[1], preferred_element_type=jnp.float32).reshape(
        row_count, length, head_count, HEAD
    )
    key_vectors = jnp.dot(normed_low, attn_set[2], preferred_element_type=jnp.float32).reshape(
        row_count, length, head_count, HEAD
    )
    value_vectors = jnp.dot(normed_low, attn_set[3], preferred_element_type=jnp.float32).astype(
        jnp.bfloat16
    )
    value_vectors = value_vectors.reshape(row_count, length, head_count, HEAD)
    query_rot = rotate(queries, cosine, sine_table).astype(jnp.bfloat16)
    key_rot = rotate(key_vectors, cosine, sine_table).astype(jnp.bfloat16)
    query_heads = jnp.moveaxis(query_rot, 2, 1)
    key_heads = jnp.moveaxis(key_rot, 2, 1)
    value_heads = jnp.moveaxis(value_vectors, 2, 1)

    def row_forward(operands):
        query_row, key_row, value_row, allowed_row = operands

        def one_head(head_parts):
            return head_forward(
                head_parts[0], head_parts[1], head_parts[2], allowed_row, score_scale
            )

        return lax.map(one_head, (query_row, key_row, value_row))

    mixture, logsum = lax.map(row_forward, (query_heads, key_heads, value_heads, allowed))
    attn_low = jnp.moveaxis(mixture, 1, 2).reshape(tokens, width).astype(jnp.bfloat16)
    middle = inputs + jnp.dot(attn_low, attn_set[4], preferred_element_type=jnp.float32)
    scale_two = lax.rsqrt(jnp.mean(middle * middle, axis=-1, keepdims=True) + EPSILON)
    normed_two = middle * scale_two
    ffn_low = (normed_two * ffn_set[0].astype(jnp.float32)).astype(jnp.bfloat16)
    gate_proj = jnp.dot(ffn_low, ffn_set[1], preferred_element_type=jnp.float32)
    up_proj = jnp.dot(ffn_low, ffn_set[2], preferred_element_type=jnp.float32)
    gate_sigm = jax.nn.sigmoid(gate_proj)
    activated = gate_proj * gate_sigm
    hidden = (activated * up_proj).astype(jnp.bfloat16)
    output_full = middle + jnp.dot(hidden, ffn_set[3], preferred_element_type=jnp.float32)
    output = output_full.astype(jnp.bfloat16).reshape(row_count, length, width)
    grad_out = cotangent.reshape(tokens, width).astype(jnp.float32)
    grad_low = grad_out.astype(jnp.bfloat16)
    down_grad = jnp.einsum("tf,td->fd", hidden, grad_low, preferred_element_type=jnp.float32)
    grad_hidden = jnp.einsum("td,fd->tf", grad_low, ffn_set[3], preferred_element_type=jnp.float32)
    gate_grad_low = (
        grad_hidden * up_proj * gate_sigm * (1.0 + gate_proj * (1.0 - gate_sigm))
    ).astype(jnp.bfloat16)
    up_grad_low = (grad_hidden * activated).astype(jnp.bfloat16)
    gate_grad = jnp.einsum("td,tf->df", ffn_low, gate_grad_low, preferred_element_type=jnp.float32)
    up_grad = jnp.einsum("td,tf->df", ffn_low, up_grad_low, preferred_element_type=jnp.float32)
    grad_normed_two = jnp.einsum(
        "tf,df->td", gate_grad_low, ffn_set[1], preferred_element_type=jnp.float32
    )
    grad_normed_two = grad_normed_two + jnp.einsum(
        "tf,df->td", up_grad_low, ffn_set[2], preferred_element_type=jnp.float32
    )
    gain_two_grad = jnp.sum(grad_normed_two * normed_two, axis=0)
    grad_middle = grad_out + norm_backward(
        grad_normed_two, normed_two, scale_two, ffn_set[0].astype(jnp.float32)
    )
    ffn_parts = (
        lax.psum_scatter(gain_two_grad, "fsdp", scatter_dimension=0, tiled=True),
        lax.psum_scatter(gate_grad, "fsdp", scatter_dimension=0, tiled=True),
        lax.psum_scatter(up_grad, "fsdp", scatter_dimension=0, tiled=True),
        lax.psum_scatter(down_grad, "fsdp", scatter_dimension=0, tiled=True),
    )
    branch_low = grad_middle.astype(jnp.bfloat16)
    out_grad = jnp.einsum("te,td->ed", attn_low, branch_low, preferred_element_type=jnp.float32)
    grad_attn = jnp.einsum(
        "td,ed->te", branch_low, attn_set[4], preferred_element_type=jnp.float32
    ).astype(jnp.bfloat16)
    grad_heads = jnp.moveaxis(grad_attn.reshape(row_count, length, head_count, HEAD), 2, 1)

    def row_backward(operands):
        query_row, key_row, value_row, grad_row, logsum_row, allowed_row = operands

        def one_head(head_parts):
            return head_backward(
                head_parts[0],
                head_parts[1],
                head_parts[2],
                head_parts[3],
                head_parts[4],
                allowed_row,
                score_scale,
            )

        return lax.map(one_head, (query_row, key_row, value_row, grad_row, logsum_row))

    grad_query_heads, grad_key_heads, grad_value_heads = lax.map(
        row_backward, (query_heads, key_heads, value_heads, grad_heads, logsum, allowed)
    )
    query_grad_low = (
        unrotate(jnp.moveaxis(grad_query_heads, 1, 2), cosine, sine_table)
        .reshape(tokens, width)
        .astype(jnp.bfloat16)
    )
    key_grad_low = (
        unrotate(jnp.moveaxis(grad_key_heads, 1, 2), cosine, sine_table)
        .reshape(tokens, width)
        .astype(jnp.bfloat16)
    )
    value_grad_low = (
        jnp.moveaxis(grad_value_heads, 1, 2).reshape(tokens, width).astype(jnp.bfloat16)
    )
    query_grad = jnp.einsum(
        "td,te->de", normed_low, query_grad_low, preferred_element_type=jnp.float32
    )
    key_grad = jnp.einsum("td,te->de", normed_low, key_grad_low, preferred_element_type=jnp.float32)
    value_grad = jnp.einsum(
        "td,te->de", normed_low, value_grad_low, preferred_element_type=jnp.float32
    )
    grad_normed_one = jnp.einsum(
        "te,de->td", query_grad_low, attn_set[1], preferred_element_type=jnp.float32
    )
    grad_normed_one = grad_normed_one + jnp.einsum(
        "te,de->td", key_grad_low, attn_set[2], preferred_element_type=jnp.float32
    )
    grad_normed_one = grad_normed_one + jnp.einsum(
        "te,de->td", value_grad_low, attn_set[3], preferred_element_type=jnp.float32
    )
    gain_one_grad = jnp.sum(grad_normed_one * normed_one, axis=0)
    input_full = grad_middle + norm_backward(
        grad_normed_one, normed_one, scale_one, attn_set[0].astype(jnp.float32)
    )
    input_grad = input_full.astype(jnp.bfloat16).reshape(row_count, length, width)
    attn_parts = (
        lax.psum_scatter(gain_one_grad, "fsdp", scatter_dimension=0, tiled=True),
        lax.psum_scatter(query_grad, "fsdp", scatter_dimension=0, tiled=True),
        lax.psum_scatter(key_grad, "fsdp", scatter_dimension=0, tiled=True),
        lax.psum_scatter(value_grad, "fsdp", scatter_dimension=0, tiled=True),
        lax.psum_scatter(out_grad, "fsdp", scatter_dimension=0, tiled=True),
    )
    every = attn_parts + ffn_parts
    return (
        output,
        input_grad,
        every[0],
        every[1],
        every[2],
        every[3],
        every[4],
        every[5],
        every[6],
        every[7],
        every[8],
    )


def solution(mesh):
    placed = (
        P("fsdp", None, None),
        P("fsdp", None),
        P("fsdp"),
        P("fsdp", None),
        P("fsdp", None),
        P("fsdp", None),
        P("fsdp", None),
        P("fsdp"),
        P("fsdp", None),
        P("fsdp", None),
        P("fsdp", None),
        P("fsdp", None, None),
    )
    return jax.shard_map(
        per_device,
        mesh=mesh,
        in_specs=placed,
        out_specs=(
            P("fsdp", None, None),
            P("fsdp", None, None),
            P("fsdp"),
            P("fsdp", None),
            P("fsdp", None),
            P("fsdp", None),
            P("fsdp", None),
            P("fsdp"),
            P("fsdp", None),
            P("fsdp", None),
            P("fsdp", None),
        ),
        check_vma=False,
    )
```

profile of v0, /device:TPU:0, one launch (start us, length us, event | category | flops | bytes accessed | tf_op | source)
XLA Modules:
  0.0 1243.9 jit_solution(14992071916210314030)
XLA Ops:
  13.9 42.1 %all-reduce.5 = (bf16[768]{0:T(1024)(128)(2,1)S(1)}, bf16[768]{0:T(1024)(128)(2,1)S(1)}) all-reduce(bf16[768]{0:T(1024)(128)(2,1)S(1)} %dynamic-update-slice, bf16[768]{0:T(1024)(128)(2,1)S(1)} %dynamic-update-slice.1), channel_id=1, replica_groups=mesh['fsdp'=32] {'fsdp'}, use_global_device_ids=true, to_apply=%add | all-reduce | flops 1536 | bytes 6144
  58.2 9.6 all-gather.10.cloned.1.call-done
  70.1 53.5 %all-gather.8.cloned.1.call-done = bf16[768,768]{1,0:T(8,128)(2,1)} async-done(((bf16[24,768]{1,0:T(8,128)(2,1)}), bf16[768,768]{1,0:T(8,128)(2,1)}) %all-gather.8.cloned.1.call-update) | async-done | bytes 1179664 | tf_op jit(solution)/shard_map/all_gather | solution.py:109
  131.6 3.9 copy.56
  138.1 41.4 %all-gather.12.cloned.1.call-done = bf16[768,768]{1,0:T(8,128)(2,1)} async-done(((bf16[24,768]{1,0:T(8,128)(2,1)}), bf16[768,768]{1,0:T(8,128)(2,1)}) %all-gather.12.cloned.1.call-update) | async-done | bytes 1179664 | tf_op jit(solution)/shard_map/all_gather | solution.py:111
  185.3 54.6 %while.50 = (s32[]{:T(128)}, bf16[12,784,64]{1,2,0:T(8,128)(2,1)}, f32[12,784]{1,0:T(8,128)S(1)}, bf16[12,784,64]{2,1,0:T(8,128)(2,1)}, bf16[12,784,64]{2,1,0:T(...) while((s32[]{:T(128)}, bf16[12,784,64]{1,2,0:T(8,128)(2,1)}, ...), condition=%wide.region_6.7_spmd.clone.clone, body=%wide.region_3.6_spmd.clone.sunk.clone | while | flops 164112368 | bytes 8255313 | solution.py:153
  239.9 3.4 multiply_reduce_fusion.3
  245.1 50.8 %all-gather.16.cloned.1.call-done = bf16[768,2048]{1,0:T(8,128)(2,1)} async-done(((bf16[24,2048]{1,0:T(8,128)(2,1)}), bf16[768,2048]{1,0:T(8,128)(2,1)}) %all-gather.16.cloned.1.call-update) | async-done | bytes 3145744 | tf_op jit(solution)/shard_map/all_gather | solution.py:116
  295.9 6.4 fusion.95
  302.3 54.1 %all-gather.18.cloned.1.call-done = bf16[768,2048]{1,0:T(8,128)(2,1)} async-done(((bf16[24,2048]{1,0:T(8,128)(2,1)}), bf16[768,2048]{1,0:T(8,128)(2,1)}) %all-gather.18.cloned.1.call-update) | async-done | bytes 3145744 | tf_op jit(solution)/shard_map/all_gather | solution.py:117
  356.4 6.8 fusion.96
  363.2 53.8 %all-gather.20.cloned.1.call-done = bf16[2048,768]{1,0:T(8,128)(2,1)} async-done(((bf16[64,768]{1,0:T(8,128)(2,1)}), bf16[2048,768]{1,0:T(8,128)(2,1)}) %all-gather.20.cloned.1.call-update) | async-done | bytes 3145744 | tf_op jit(solution)/shard_map/all_gather | solution.py:118
  417.0 9.8 multiply_convert_fusion.1
  431.8 3.1 multiply_reduce_fusion.1
  439.9 3.8 convolution_convert_fusion
  446.5 114.9 %while.51 = (s32[]{:T(128)}, f32[12,784,64]{1,2,0:T(8,128)}, f32[12,784,64]{1,2,0:T(8,128)}, bf16[12,784,64]{1,2,0:T(8,128)(2,1)S(1)}, bf16[12,784,64]{2,1,0:T(8...) while((s32[]{:T(128)}, f32[12,784,64]{1,2,0:T(8,128)}, ...), condition=%wide.region_11.12_spmd.clone.clone, body=%wide.region_9.11_spmd.clone.sunk.clone | while | flops 400855296 | bytes 20741992 | solution.py:215
  561.4 4.2 multiply_add_fusion.1
  567.2 3.1 fusion.81
  576.2 4.4 fusion.79
  580.7 7.3 fusion.100
  588.0 7.3 fusion.101
  596.6 8.0 fusion.71
  610.5 3.3 fusion.64
  613.8 38.6 %all-reduce.4 = (f32[768]{0:T(1024)S(1)}, f32[768]{0:T(1024)S(1)}) all-reduce(f32[768]{0:T(1024)S(1)} %get-tuple-element.269, f32[768]{0:T(1024)S(1)} %get-tuple-element.267), channel_id=2, replica_groups=mesh['fsdp'=32] {'fsdp'}, use_global_device_ids=true, to_apply=%region_14.15.clone | all-reduce | flops 1536 | bytes 12288
  653.5 4.3 fusion.69
  657.8 5.6 fusion.68
  663.4 5.0 reduce-scatter.10.cloned.1.call-done
  668.4 103.8 %reduce-scatter.8.cloned.1.call-done = f32[24,768]{1,0:T(8,128)} async-done(((f32[768,768]{1,0:T(8,128)}), f32[24,768]{1,0:T(8,128)}) %reduce-scatter.8.cloned.1.call-update) | async-done | bytes 73744 | tf_op jit(solution)/shard_map/reduce_scatter | solution.py:256
  772.2 104.7 %reduce-scatter.12.cloned.1.call-done = f32[24,768]{1,0:T(8,128)} async-done(((f32[768,768]{1,0:T(8,128)}), f32[24,768]{1,0:T(8,128)}) %reduce-scatter.12.cloned.1.call-update) | async-done | bytes 73744 | tf_op jit(solution)/shard_map/reduce_scatter | solution.py:258
  876.9 119.7 %reduce-scatter.16.cloned.1.call-done = f32[24,2048]{1,0:T(8,128)} async-done(((f32[768,2048]{1,0:T(8,128)}), f32[24,2048]{1,0:T(8,128)}) %reduce-scatter.16.cloned.1.call-update) | async-done | bytes 196624 | tf_op jit(solution)/shard_map/reduce_scatter | solution.py:190
  996.6 120.9 %reduce-scatter.18.cloned.1.call-done = f32[24,2048]{1,0:T(8,128)} async-done(((f32[768,2048]{1,0:T(8,128)}), f32[24,2048]{1,0:T(8,128)}) %reduce-scatter.18.cloned.1.call-update) | async-done | bytes 196624 | tf_op jit(solution)/shard_map/reduce_scatter | solution.py:191
  1117.5 119.6 %reduce-scatter.20.cloned.1.call-done = f32[64,768]{1,0:T(8,128)} async-done(((f32[2048,768]{1,0:T(8,128)}), f32[64,768]{1,0:T(8,128)}) %reduce-scatter.20.cloned.1.call-update) | async-done | bytes 196624 | tf_op jit(solution)/shard_map/reduce_scatter | solution.py:192
  (282 shorter events, 226.1 us)
Async XLA Ops:
  7.2 48.8 %copy-start.2 = (bf16[1,784,768]{2,1,0:T(8,128)(2,1)S(1)}, bf16[1,784,768]{2,1,0:T(8,128)(2,1)}, u32[]{:S(2)}) copy-start(bf16[1,784,768]{2,1,0:T(8,128)(2,1)} %param.16) | copy-start | bytes 3612676
  7.2 49.1 %copy-start.21 = (s32[1,784]{1,0:T(1,128)S(1)}, s32[1,784]{1,0:T(1,128)}, u32[]{:S(2)}) copy-start(s32[1,784]{1,0:T(1,128)} %param.17) | copy-start | bytes 9412
  7.2 60.5 %all-gather.10.cloned.1.call-start = ((), (), s32[]{:S(2)}) async-start(), calls=%async_computation.8 | async-start | bytes 1216512 | tf_op jit(solution)/shard_map/all_gather | solution.py:110
  7.9 115.7 %all-gather.8.cloned.1.call-start = ((), (), s32[]{:S(2)}) async-start(), calls=%async_computation.7 | async-start | bytes 1216512 | tf_op jit(solution)/shard_map/all_gather | solution.py:109
  8.7 170.8 %all-gather.12.cloned.1.call-start = ((), (), s32[]{:S(2)}) async-start(), calls=%async_computation.9 | async-start | bytes 1216512 | tf_op jit(solution)/shard_map/all_gather | solution.py:111
  9.4 230.5 %all-gather.14.cloned.1.call-start = ((), (), s32[]{:S(2)}) async-start(), calls=%async_computation.10 | async-start | bytes 1216512 | tf_op jit(solution)/shard_map/all_gather | solution.py:112
  10.0 285.9 %all-gather.16.cloned.1.call-start = ((), (), s32[]{:S(2)}) async-start(), calls=%async_computation.11 | async-start | bytes 3244032 | tf_op jit(solution)/shard_map/all_gather | solution.py:116
  10.6 345.8 %all-gather.18.cloned.1.call-start = ((), (), s32[]{:S(2)}) async-start(), calls=%async_computation.12 | async-start | bytes 3244032 | tf_op jit(solution)/shard_map/all_gather | solution.py:117
  11.2 405.9 %all-gather.20.cloned.1.call-start = ((), (), s32[]{:S(2)}) async-start(), calls=%async_computation.13 | async-start | bytes 3244032 | tf_op jit(solution)/shard_map/all_gather | solution.py:118
  11.9 651.5 %reduce-scatter.14.cloned.1.call-start = ((), (), s32[]{:S(2)}) async-start(), calls=%async_computation.17 | async-start | bytes 2433024 | tf_op jit(solution)/shard_map/reduce_scatter | solution.py:259
  12.2 58.0 %copy-start = (bf16[12,784,64]{1,2,0:T(8,128)(2,1)}, bf16[12,784,64]{1,2,0:T(8,128)(2,1)S(1)}, u32[]{:S(2)}) copy-start(bf16[12,784,64]{1,2,0:T(8,128)(2,1)S(1)} %fusion.94) | copy-start | bytes 3612676
  302.3 114.8 %copy-start.17 = (bf16[1,784,768]{2,1,0:T(8,128)(2,1)S(1)}, bf16[1,784,768]{2,1,0:T(8,128)(2,1)}, u32[]{:S(2)}) copy-start(bf16[1,784,768]{2,1,0:T(8,128)(2,1)} %param.27) | copy-start | bytes 3612676
  417.0 9.8 copy-start.23
  426.8 2.7 copy-start.11
  426.8 3.3 copy-start.10
  426.9 3.5 copy-start.7
  426.9 4.9 copy-start.24
  434.9 2.1 copy-start.16
  437.1 2.9 copy-start.25
  439.9 228.5 %reduce-scatter.10.cloned.1.call-start = ((), (), s32[]{:S(2)}) async-start(), calls=%async_computation.15 | async-start | bytes 2433024 | tf_op jit(solution)/shard_map/reduce_scatter | solution.py:257
  443.8 2.8 copy-start.1
  570.4 201.8 %reduce-scatter.8.cloned.1.call-start = ((), (), s32[]{:S(2)}) async-start(), calls=%async_computation.14 | async-start | bytes 2433024 | tf_op jit(solution)/shard_map/reduce_scatter | solution.py:256
  570.5 2.5 copy-start.4
  576.1 300.8 %reduce-scatter.12.cloned.1.call-start = ((), (), s32[]{:S(2)}) async-start(), calls=%async_computation.16 | async-start | bytes 2433024 | tf_op jit(solution)/shard_map/reduce_scatter | solution.py:258
  580.6 415.9 %reduce-scatter.16.cloned.1.call-start = ((), (), s32[]{:S(2)}) async-start(), calls=%async_computation.18 | async-start | bytes 6488064 | tf_op jit(solution)/shard_map/reduce_scatter | solution.py:190
  588.0 529.5 %reduce-scatter.18.cloned.1.call-start = ((), (), s32[]{:S(2)}) async-start(), calls=%async_computation.19 | async-start | bytes 6488064 | tf_op jit(solution)/shard_map/reduce_scatter | solution.py:191
  595.3 641.8 %reduce-scatter.20.cloned.1.call-start = ((), (), s32[]{:S(2)}) async-start(), calls=%async_computation.20 | async-start | bytes 6488064 | tf_op jit(solution)/shard_map/reduce_scatter | solution.py:192
  606.0 2.8 copy-start.15
  606.0 2.8 copy-start.20
  608.8 1.6 copy-start.19
  653.5 4.3 copy-start.8
  653.5 4.3 copy-start.22
  (8 other events, 10.7 us)
Sparse Core Ops, SparseCore 0:
  10.9 56.7 all-gather.9
  70.6 52.9 all-gather.7
  126.5 52.9 all-gather.11
  182.3 52.9 all-gather.13
  238.0 57.8 all-gather.15
  298.6 57.7 all-gather.17
  359.3 57.7 all-gather.19
  440.0 97.8 reduce-scatter.13
  570.5 97.8 reduce-scatter.9
  674.1 98.0 reduce-scatter.7
  779.0 97.8 reduce-scatter.11
  883.0 113.5 reduce-scatter.15
  1003.7 113.7 reduce-scatter.17
  1123.5 113.5 reduce-scatter.19
where the time goes:
time: 1260 us; the launch traced here: 1240 us
  waiting for transfers between devices  841 us (67%)
  matrix products  248 us (20%)
  blocking collectives  80.7 us (6%)
  local copies, waits for them, and re-layouts  32.2 us (3%)
  other arithmetic  25.2 us (2%)
  between operations  14.5 us (1%)
    reduce_scatter x1, waiting for transfers between devices, per_device(): lax.psum_scatter(up_grad, 'fsdp', scatter_dimension=0, tiled=True)  121 us
    reduce_scatter x1, waiting for transfers between devices, per_device(): lax.psum_scatter(gate_grad, 'fsdp', scatter_dimension=0, tiled=True)  120 us
    reduce_scatter x1, waiting for transfers between devices, per_device(): lax.psum_scatter(down_grad, 'fsdp', scatter_dimension=0, tiled=True)  120 us
    reduce_scatter x1, waiting for transfers between devices, per_device(): lax.psum_scatter(value_grad, 'fsdp', scatter_dimension=0, tiled=True)  105 us
    reduce_scatter x1, waiting for transfers between devices, per_device(): lax.psum_scatter(query_grad, 'fsdp', scatter_dimension=0, tiled=True)  104 us
    unnamed x2, blocking collectives  80.7 us
    all_gather x1, waiting for transfers between devices, per_device(): lax.all_gather(w_up, 'fsdp', axis=0, tiled=True)  54.1 us
    all_gather x1, waiting for transfers between devices, per_device(): lax.all_gather(w_down, 'fsdp', axis=0, tiled=True)  53.8 us
  transfers between devices with their start and end apart: 14, of which 12 were waited for; matrix products, arithmetic and copies ran while one was open for 22% of the time, Pallas kernels for 0%

commit v1 on v0

--- a/solution.py
+++ b/solution.py
@@ -6,6 +6,18 @@
 
 HEAD = 64
 EPSILON = 1e-05
+
+
+def gather_by_bits(shard, axis, dim):
+    ways, here, step = (lax.axis_size(axis), lax.axis_index(axis), shard.shape[dim])
+    line, have = (shard, 1)
+    while have < ways:
+        line = jnp.concatenate(
+            [line, lax.ppermute(line, axis, [(d, (d - have) % ways) for d in range(ways)])],
+            axis=dim,
+        )
+        have = 2 * have
+    return jnp.roll(line, here * step, axis=dim)
 
 
 def rope_tables(segment_row, head_size):
@@ -108,7 +120,7 @@
         lax.all_gather(gain_attn, "fsdp", axis=0, tiled=True),
         lax.all_gather(w_query, "fsdp", axis=0, tiled=True),
         lax.all_gather(w_key, "fsdp", axis=0, tiled=True),
-        lax.all_gather(w_value, "fsdp", axis=0, tiled=True),
+        gather_by_bits(w_value, "fsdp", 0),
         lax.all_gather(w_out, "fsdp", axis=0, tiled=True),
     )
     ffn_set = (

time: 1260 us -> 1220 us (0.968)
  waiting for transfers between devices: 841 us -> 746 us
  local copies, waits for them, and re-layouts: 32.2 us -> 65.7 us
  blocking collectives: 80.7 us -> 94.1 us
    all_gather x1 -> x0, waiting for transfers between devices: 41.4 us -> none  [per_device(): lax.all_gather(w_value, 'fsdp', axis=0, tiled=True)]
    all_gather x1, waiting for transfers between devices: 53.5 us -> 16.2 us  [per_device(): lax.all_gather(w_query, 'fsdp', axis=0, tiled=True)]
    all_gather x1, waiting for transfers between devices: 54.1 us -> 32 us  [per_device(): lax.all_gather(w_up, 'fsdp', axis=0, tiled=True)]
    dynamic_update_slice x12, local copies, waits for them, and re-layouts: 1.19 us -> 16.6 us  [row_forward(): return lax.map(one_head, (query_row, key_row, value_row))]
    ppermute x0 -> x5, waiting for transfers between devices: none -> 13.6 us  [gather_by_bits(): lax.ppermute(line, axis, [(d, (d - have) % ways) for d in range(ways)])]
    unnamed x2, blocking collectives: 80.7 us -> 94.1 us
    unnamed x62 -> x88, local copies, waits for them, and re-layouts: 23.2 us -> 30.4 us
  transfers between devices with their start and end apart: 14 -> 18, of which waited for: 12 -> 13; matrix products, arithmetic and copies ran while one was open for 22% -> 26% of each run, Pallas kernels for 0% -> 0%
where the time goes in v1:
time: 1220 us; the launch traced here: 1210 us
  waiting for transfers between devices  746 us (61%)
  matrix products  250 us (20%)
  blocking collectives  94.1 us (8%)
  local copies, waits for them, and re-layouts  65.7 us (5%)
  other arithmetic  29.7 us (2%)
  between operations  14.6 us (1%)
    reduce_scatter x1, waiting for transfers between devices, per_device(): lax.psum_scatter(gate_grad, 'fsdp', scatter_dimension=0, tiled=True)  121 us
    reduce_scatter x1, waiting for transfers between devices, per_device(): lax.psum_scatter(down_grad, 'fsdp', scatter_dimension=0, tiled=True)  120 us
    reduce_scatter x1, waiting for transfers between devices, per_device(): lax.psum_scatter(up_grad, 'fsdp', scatter_dimension=0, tiled=True)  120 us
    reduce_scatter x1, waiting for transfers between devices, per_device(): lax.psum_scatter(value_grad, 'fsdp', scatter_dimension=0, tiled=True)  105 us
    reduce_scatter x1, waiting for transfers between devices, per_device(): lax.psum_scatter(query_grad, 'fsdp', scatter_dimension=0, tiled=True)  104 us
    unnamed x2, blocking collectives  94.1 us
    all_gather x1, waiting for transfers between devices, per_device(): lax.all_gather(w_gate, 'fsdp', axis=0, tiled=True)  54.1 us
    all_gather x1, waiting for transfers between devices, per_device(): lax.all_gather(w_down, 'fsdp', axis=0, tiled=True)  53.6 us
  transfers between devices with their start and end apart: 18, of which 13 were waited for; matrix products, arithmetic and copies ran while one was open for 26% of the time, Pallas kernels for 0%

profile of v1, /device:TPU:0, one launch (start us, length us, event | category | flops | bytes accessed | tf_op | source)
XLA Modules:
  0.0 1210.8 jit_solution(6549738125295511537)
XLA Ops:
  10.6 6.4 collective-permute-start
  26.3 5.0 collective-permute-done.2
  34.5 6.7 collective-permute-done.3
  43.2 55.4 %all-reduce.5 = (bf16[768]{0:T(1024)(128)(2,1)S(1)}, bf16[768]{0:T(1024)(128)(2,1)S(1)}) all-reduce(bf16[768]{0:T(1024)(128)(2,1)S(1)} %dynamic-update-slice, bf16[768]{0:T(1024)(128)(2,1)S(1)} %dynamic-update-slice.1), channel_id=1, replica_groups=mesh['fsdp'=32] {'fsdp'}, use_global_device_ids=true, to_apply=%add | all-reduce | flops 1536 | bytes 6144
  108.3 3.5 convolution_convert_fusion.1
  120.7 16.2 %all-gather.7.cloned.1.call-done = bf16[768,768]{1,0:T(8,128)(2,1)} async-done(((bf16[24,768]{1,0:T(8,128)(2,1)}), bf16[768,768]{1,0:T(8,128)(2,1)}) %all-gather.7.cloned.1.call-update) | async-done | bytes 1179664 | tf_op jit(solution)/shard_map/all_gather | solution.py:121
  146.6 69.8 %while.50 = (s32[]{:T(128)}, bf16[12,784,64]{1,2,0:T(8,128)(2,1)}, f32[12,784]{1,0:T(8,128)}, bf16[12,784,64]{2,1,0:T(8,128)(2,1)}, bf16[12,784,64]{2,1,0:T(8,12...) while((s32[]{:T(128)}, bf16[12,784,64]{1,2,0:T(8,128)(2,1)}, ...), condition=%wide.region_6.7_spmd.clone.clone, body=%wide.region_3.6_spmd.clone.sunk.clone | while | flops 164112368 | bytes 8255313 | solution.py:165
  216.4 3.4 multiply_reduce_fusion.3
  221.5 32.0 %all-gather.15.cloned.1.call-done = bf16[768,2048]{1,0:T(8,128)(2,1)} async-done(((bf16[24,2048]{1,0:T(8,128)(2,1)}), bf16[768,2048]{1,0:T(8,128)(2,1)}) %all-gather.15.cloned.1.call-update) | async-done | bytes 3145744 | tf_op jit(solution)/shard_map/all_gather | solution.py:129
  253.5 6.4 fusion.100
  259.9 54.1 %all-gather.13.cloned.1.call-done = bf16[768,2048]{1,0:T(8,128)(2,1)} async-done(((bf16[24,2048]{1,0:T(8,128)(2,1)}), bf16[768,2048]{1,0:T(8,128)(2,1)}) %all-gather.13.cloned.1.call-update) | async-done | bytes 3145744 | tf_op jit(solution)/shard_map/all_gather | solution.py:128
  314.0 6.9 fusion.99
  320.9 53.6 %all-gather.17.cloned.1.call-done = bf16[2048,768]{1,0:T(8,128)(2,1)} async-done(((bf16[64,768]{1,0:T(8,128)(2,1)}), bf16[2048,768]{1,0:T(8,128)(2,1)}) %all-gather.17.cloned.1.call-update) | async-done | bytes 3145744 | tf_op jit(solution)/shard_map/all_gather | solution.py:130
  374.5 9.8 multiply_convert_fusion.1
  397.5 3.8 convolution_convert_fusion
  404.1 123.8 %while.51 = (s32[]{:T(128)}, f32[12,784,64]{1,2,0:T(8,128)}, f32[12,784,64]{1,2,0:T(8,128)}, bf16[12,784,64]{1,2,0:T(8,128)(2,1)S(1)}, bf16[12,784,64]{2,1,0:T(8...) while((s32[]{:T(128)}, f32[12,784,64]{1,2,0:T(8,128)}, ...), condition=%wide.region_11.12_spmd.clone.clone, body=%wide.region_9.11_spmd.clone.sunk.clone | while | flops 400855296 | bytes 20741992 | solution.py:227
  527.9 4.2 multiply_add_fusion.1
  533.7 3.2 fusion.81
  542.7 4.4 fusion.79
  547.2 7.3 fusion.105
  554.5 7.3 fusion.104
  563.1 8.1 fusion.71
  577.5 3.3 fusion.64
  580.8 38.7 %all-reduce.4 = (f32[768]{0:T(1024)S(1)}, f32[768]{0:T(1024)S(1)}) all-reduce(f32[768]{0:T(1024)S(1)} %get-tuple-element.269, f32[768]{0:T(1024)S(1)} %get-tuple-element.267), channel_id=2, replica_groups=mesh['fsdp'=32] {'fsdp'}, use_global_device_ids=true, to_apply=%region_14.15.clone | all-reduce | flops 1536 | bytes 12288
  620.7 4.3 fusion.69
  624.9 5.6 fusion.68
  630.5 4.6 reduce-scatter.10.cloned.1.call-done
  635.1 103.9 %reduce-scatter.8.cloned.1.call-done = f32[24,768]{1,0:T(8,128)} async-done(((f32[768,768]{1,0:T(8,128)}), f32[24,768]{1,0:T(8,128)}) %reduce-scatter.8.cloned.1.call-update) | async-done | bytes 73744 | tf_op jit(solution)/shard_map/reduce_scatter | solution.py:268
  739.0 104.6 %reduce-scatter.12.cloned.1.call-done = f32[24,768]{1,0:T(8,128)} async-done(((f32[768,768]{1,0:T(8,128)}), f32[24,768]{1,0:T(8,128)}) %reduce-scatter.12.cloned.1.call-update) | async-done | bytes 73744 | tf_op jit(solution)/shard_map/reduce_scatter | solution.py:270
  843.6 119.8 %reduce-scatter.18.cloned.1.call-done = f32[24,2048]{1,0:T(8,128)} async-done(((f32[768,2048]{1,0:T(8,128)}), f32[24,2048]{1,0:T(8,128)}) %reduce-scatter.18.cloned.1.call-update) | async-done | bytes 196624 | tf_op jit(solution)/shard_map/reduce_scatter | solution.py:203
  963.4 120.7 %reduce-scatter.16.cloned.1.call-done = f32[24,2048]{1,0:T(8,128)} async-done(((f32[768,2048]{1,0:T(8,128)}), f32[24,2048]{1,0:T(8,128)}) %reduce-scatter.16.cloned.1.call-update) | async-done | bytes 196624 | tf_op jit(solution)/shard_map/reduce_scatter | solution.py:202
  1084.1 119.9 %reduce-scatter.20.cloned.1.call-done = f32[64,768]{1,0:T(8,128)} async-done(((f32[2048,768]{1,0:T(8,128)}), f32[64,768]{1,0:T(8,128)}) %reduce-scatter.20.cloned.1.call-update) | async-done | bytes 196624 | tf_op jit(solution)/shard_map/reduce_scatter | solution.py:204
  (320 shorter events, 272.4 us)
Async XLA Ops:
  7.2 24.1 %copy-start.23 = (bf16[24,768]{1,0:T(8,128)(2,1)S(1)}, bf16[24,768]{1,0:T(8,128)(2,1)}, u32[]{:S(2)}) copy-start(bf16[24,768]{1,0:T(8,128)(2,1)} %param.21) | copy-start | bytes 110596
  7.2 109.0 %all-gather.9.cloned.1.call-start = ((), (), s32[]{:S(2)}) async-start(), calls=%async_computation.8 | async-start | bytes 1216512 | tf_op jit(solution)/shard_map/all_gather | solution.py:122
  7.9 129.0 %all-gather.7.cloned.1.call-start = ((), (), s32[]{:S(2)}) async-start(), calls=%async_computation.7 | async-start | bytes 1216512 | tf_op jit(solution)/shard_map/all_gather | solution.py:121
  8.7 207.7 %all-gather.11.cloned.1.call-start = ((), (), s32[]{:S(2)}) async-start(), calls=%async_computation.9 | async-start | bytes 1216512 | tf_op jit(solution)/shard_map/all_gather | solution.py:124
  9.4 244.1 %all-gather.15.cloned.1.call-start = ((), (), s32[]{:S(2)}) async-start(), calls=%async_computation.11 | async-start | bytes 3244032 | tf_op jit(solution)/shard_map/all_gather | solution.py:129
  10.0 304.0 %all-gather.13.cloned.1.call-start = ((), (), s32[]{:S(2)}) async-start(), calls=%async_computation.10 | async-start | bytes 3244032 | tf_op jit(solution)/shard_map/all_gather | solution.py:128
  10.6 363.9 %all-gather.17.cloned.1.call-start = ((), (), s32[]{:S(2)}) async-start(), calls=%async_computation.12 | async-start | bytes 3244032 | tf_op jit(solution)/shard_map/all_gather | solution.py:130
  10.6 8.9 collective-permute-start
  17.1 613.5 %reduce-scatter.14.cloned.1.call-start = ((), (), s32[]{:S(2)}) async-start(), calls=%async_computation.16 | async-start | bytes 2433024 | tf_op jit(solution)/shard_map/reduce_scatter | solution.py:271
  18.7 24.0 %copy-start.32 = (bf16[24]{0:T(256)(128)(2,1)S(1)}, bf16[24]{0:T(256)(128)(2,1)}, u32[]{:S(2)}) copy-start(bf16[24]{0:T(256)(128)(2,1)} %param.18) | copy-start | bytes 148
  18.7 24.2 %copy-start.33 = (bf16[24]{0:T(256)(128)(2,1)S(1)}, bf16[24]{0:T(256)(128)(2,1)}, u32[]{:S(2)}) copy-start(bf16[24]{0:T(256)(128)(2,1)} %param.23) | copy-start | bytes 148
  19.5 80.2 %copy-start.26 = (s32[784]{0:T(1024)}, s32[784]{0:T(1024)S(1)}, u32[]{:S(2)}) copy-start(s32[784]{0:T(1024)S(1)} %reduce.3) | copy-start | bytes 9412
  19.5 80.2 %copy-start.24 = (bf16[24,768]{1,0:T(8,128)(2,1)}, bf16[24,768]{1,0:T(8,128)(2,1)S(1)}, u32[]{:S(2)}) copy-start(bf16[24,768]{1,0:T(8,128)(2,1)S(1)} %collective-permute-done) | copy-start | bytes 110596
  20.3 4.4 collective-permute-start.1
  25.4 5.8 collective-permute-start.2
  26.3 73.3 %copy-start = (bf16[12,784,64]{1,2,0:T(8,128)(2,1)}, bf16[12,784,64]{1,2,0:T(8,128)(2,1)S(1)}, u32[]{:S(2)}) copy-start(bf16[12,784,64]{1,2,0:T(8,128)(2,1)S(1)} %fusion.98) | copy-start | bytes 3612676
  31.3 10.0 collective-permute-start.3
  41.3 57.3 %copy-start.20 = (bf16[192,768]{1,0:T(8,128)(2,1)}, bf16[192,768]{1,0:T(8,128)(2,1)S(1)}, u32[]{:S(2)}) copy-start(bf16[192,768]{1,0:T(8,128)(2,1)S(1)} %collective-permute-done.3) | copy-start | bytes 884740
  42.2 59.4 %collective-permute-start.4 = (bf16[384,768]{1,0:T(8,128)(2,1)}, bf16[384,768]{1,0:T(8,128)(2,1)S(1)}, u32[]{:S(2)}, u32[]{:S(2)}) collective-permute-start(bf16[384,768]{1,0:T(8,128)(2,1)} %get-tuple-element.326), channel_id=1, source_target_pairs={{0,16},{1,17},{2,18},{3,19},{4,20},{5,21},{6,22},{7,23},{8,24},{9,... | collective-permute-start | bytes 1769480 | tf_op jit(solution)/shard_map/ppermute | solution.py:16
  99.6 8.7 copy-start.2
  259.9 114.6 %copy-start.18 = (bf16[1,784,768]{2,1,0:T(8,128)(2,1)S(1)}, bf16[1,784,768]{2,1,0:T(8,128)(2,1)}, u32[]{:S(2)}) copy-start(bf16[1,784,768]{2,1,0:T(8,128)(2,1)} %param.27) | copy-start | bytes 3612676
  374.5 9.9 copy-start.30
  384.3 3.5 copy-start.7
  384.4 4.9 copy-start.29
  397.5 237.6 %reduce-scatter.10.cloned.1.call-start = ((), (), s32[]{:S(2)}) async-start(), calls=%async_computation.14 | async-start | bytes 2433024 | tf_op jit(solution)/shard_map/reduce_scatter | solution.py:269
  536.9 202.0 %reduce-scatter.8.cloned.1.call-start = ((), (), s32[]{:S(2)}) async-start(), calls=%async_computation.13 | async-start | bytes 2433024 | tf_op jit(solution)/shard_map/reduce_scatter | solution.py:268
  542.6 301.0 %reduce-scatter.12.cloned.1.call-start = ((), (), s32[]{:S(2)}) async-start(), calls=%async_computation.15 | async-start | bytes 2433024 | tf_op jit(solution)/shard_map/reduce_scatter | solution.py:270
  547.1 416.2 %reduce-scatter.18.cloned.1.call-start = ((), (), s32[]{:S(2)}) async-start(), calls=%async_computation.18 | async-start | bytes 6488064 | tf_op jit(solution)/shard_map/reduce_scatter | solution.py:203
  554.5 529.6 %reduce-scatter.16.cloned.1.call-start = ((), (), s32[]{:S(2)}) async-start(), calls=%async_computation.17 | async-start | bytes 6488064 | tf_op jit(solution)/shard_map/reduce_scatter | solution.py:202
  561.9 642.2 %reduce-scatter.20.cloned.1.call-start = ((), (), s32[]{:S(2)}) async-start(), calls=%async_computation.19 | async-start | bytes 6488064 | tf_op jit(solution)/shard_map/reduce_scatter | solution.py:204
  620.7 4.3 copy-start.8
  620.7 4.3 copy-start.28
  (20 other events, 40.8 us)
Sparse Core Ops, SparseCore 0:
  10.9 69.2 all-gather.8
  83.1 53.7 all-gather.6
  139.8 52.9 all-gather.10
  195.6 57.8 all-gather.14
  256.2 57.7 all-gather.12
  316.7 57.7 all-gather.16
  397.6 97.8 reduce-scatter.13
  537.1 97.9 reduce-scatter.9
  641.0 97.9 reduce-scatter.7
  745.5 98.0 reduce-scatter.11
  849.8 113.4 reduce-scatter.17
  970.4 113.6 reduce-scatter.15
  1090.3 113.6 reduce-scatter.19
